TPU v7x, 256 devices: a whole 4x4x8 slice. The times are simulated.
256 devices in a mesh: tile: 16 (over z, core), bank: 16 (over y, x).
Axes of the slice: x: 4, y: 4, z: 8, core: 2. Of those that a mesh axis runs over, the one named last changes fastest.
Arguments:
- volume: bfloat16 [1024, 1024, 128], P('tile', 'bank'), may hold values from -6 to 6
- pick_list: int32 [3, 16, 16, 16], P(None, 'tile', 'bank'), may hold values from 0 to 1023, as said below
- box_counts: int32 [16, 16], P('tile', 'bank'), may hold values from 1 to 16, as said below
- orientations: int32 [16, 16, 16, 128], P('tile', 'bank'), may hold values from 0 to 255, all different within a row
- orient_weight: int32 [16, 16, 16, 128], P('tile', 'bank'), may hold values from 1 to 4
- reference_bank: bfloat16 [256, 20, 4096], P('bank'), may hold values from -6 to 6
Outputs:
- class_sums: float32 [256, 20, 4096], P('bank')
- weight_sums: float32 [256, 20], P('bank')
Inputs may be any that keep to these rules, and one draw needn't show every extreme that they name: pick_list[0, t, b, s] lies in [t * 64, (t + 1) * 64), pick_list[1, t, b, s] in [b * 64, (b + 1) * 64), and pick_list[2, t, b, s] in [0, 32]. `box_counts`: every device has at least one live slot and some device has all 16. The 128 orientations of a slot are distinct.
All inputs are finite; a program needn't handle non-finite values.
Results may differ from a plain program's by a relative error of at most 0.012.
Values may be sent and summed in bfloat16 or wider, within the bound.
A program may use at most 128 MiB of HBM per device.

v0:
```python
import jax
import jax.numpy as jnp
from jax import lax
from jax.sharding import PartitionSpec as P

B = 96
L = 16
R = 256
F = 4096
EPSILON = 1e-06


def extended(block, sides, width):
    for axis, dim in sides:
        count = lax.axis_size(axis)
        forward = [(i, i + 1) for i in range(count - 1)]
        backward = [(target, source) for source, target in forward]
        low = lax.ppermute(
            lax.slice_in_dim(block, block.shape[dim] - width, None, axis=dim), axis, forward
        )
        high = lax.ppermute(lax.slice_in_dim(block, 0, width, axis=dim), axis, backward)
        block = jnp.concatenate([low, block, high], axis=dim)
    return block


def fourier_table():
    samples = jnp.arange(B).astype(jnp.float32)
    terms = jnp.arange(L)
    frequency = jnp.where(terms <= L // 2, terms, terms - L // 2).astype(jnp.float32)
    angles = 2.0 * jnp.pi * frequency[:, None] * samples[None, :] / B
    table = jnp.where((terms <= L // 2)[:, None], jnp.cos(angles), jnp.sin(angles)) / jnp.sqrt(
        jnp.float32(B)
    )
    table_half = table.astype(jnp.bfloat16)
    return (table_half, table_half.astype(jnp.float32))


def box_features(box_cube, table_half, table_full):
    first = jnp.dot(
        box_cube.reshape(B * B, B), table_half.T, preferred_element_type=jnp.float32
    ).reshape(B, B, L)
    second = jnp.einsum("xyc,by->xbc", first, table_full, precision=lax.Precision.HIGHEST)
    third = jnp.einsum("xbc,ax->abc", second, table_full, precision=lax.Precision.HIGHEST)
    return third.reshape(L * L * L).astype(jnp.bfloat16)


def norms_of(features):
    feature_wide = features.astype(jnp.float32)
    return jnp.sqrt(jnp.mean(feature_wide * feature_wide, axis=1) + EPSILON)


def correlate(features, box_norm, bank_rows):
    scores = jnp.einsum("if,rcf->irc", features, bank_rows, preferred_element_type=jnp.float32)
    bank_wide = bank_rows.astype(jnp.float32)
    ref_norm = jnp.sqrt(jnp.mean(bank_wide * bank_wide, axis=2) + EPSILON)
    return scores / (F * box_norm[:, None, None] * ref_norm[None])


def accumulate(multiplicity, correl, features):
    weights = (multiplicity.astype(jnp.float32)[:, :, None] * jnp.maximum(correl, 0.0)).astype(
        jnp.bfloat16
    )
    class_sums = jnp.einsum("irc,if->rcf", weights, features, preferred_element_type=jnp.float32)
    weight_sums = jnp.sum(weights.astype(jnp.float32), axis=0)
    return (class_sums, weight_sums)


def score_local(box_rows, box_multiplicity, reference_bank):
    local_rows = reference_bank.shape[0]
    row_start = lax.axis_index("bank") * local_rows
    local_multiplicity = lax.dynamic_slice_in_dim(box_multiplicity, row_start, local_rows, 1)
    box_norm = norms_of(box_rows)
    correl = correlate(box_rows, box_norm, reference_bank)
    return accumulate(local_multiplicity, correl, box_rows)


def body(volume, pick_list, box_counts, orientations, orient_weight, reference_bank):
    table_half, table_full = fourier_table()
    half_box = B // 2
    padded = extended(volume, (("tile", 0), ("bank", 1)), half_box)
    offset_x = lax.axis_index("tile") * volume.shape[0]
    offset_y = lax.axis_index("bank") * volume.shape[1]
    coords = jnp.stack(
        [pick_list[0, 0, 0] - offset_x, pick_list[1, 0, 0] - offset_y, pick_list[2, 0, 0]], axis=1
    )

    def extract_one(corner):
        box_cube = lax.dynamic_slice(padded, (corner[0], corner[1], corner[2]), (B, B, B))
        return box_features(box_cube, table_half, table_full)

    features = lax.map(extract_one, coords)
    slots = pick_list.shape[3]
    live_slots = jnp.arange(slots) < box_counts[0, 0]
    matches = orientations[0, 0][:, :, None] == jnp.arange(R)[None, None, :]
    multiplicity = jnp.sum(
        jnp.where(matches, orient_weight[0, 0][:, :, None].astype(jnp.float32), 0.0), axis=1
    )
    multiplicity = jnp.where(live_slots[:, None], multiplicity, 0.0).astype(jnp.bfloat16)
    group_features, group_multiplicity = (
        lax.all_gather(features, "bank", axis=0, tiled=True),
        lax.all_gather(multiplicity, "bank", axis=0, tiled=True),
    )
    class_sums, weight_sums = score_local(group_features, group_multiplicity, reference_bank)
    class_sums, weight_sums = lax.psum((class_sums, weight_sums), "tile")
    return (class_sums, weight_sums)


def solution(mesh):
    in_specs = (
        P("tile", "bank", None),
        P(None, "tile", "bank", None),
        P("tile", "bank"),
        P("tile", "bank", None, None),
        P("tile", "bank", None, None),
        P("bank", None, None),
    )
    out_specs = (P("bank", None, None), P("bank", None))
    return jax.shard_map(body, mesh=mesh, in_specs=in_specs, out_specs=out_specs, check_vma=False)
```

profile of v0, /device:TPU:2, one launch (start us, length us, event | category | flops | bytes accessed | tf_op | source)
XLA Modules:
  0.0 504.5 jit_solution(12485962151624641500)
XLA Ops:
  8.8 1.8 collective-permute-start
  12.7 3.8 collective-permute-done.1
  16.5 2.6 fusion.58
  19.2 3.4 collective-permute-start.2
  22.6 3.7 collective-permute-start.3
  26.4 31.6 %collective-permute-done.2 = bf16[160,48,128]{2,1,0:T(8,128)(2,1)} collective-permute-done((bf16[160,48,128]{2,1,0:T(8,128)(2,1)}, bf16[160,48,128]{2,1,0:T(8,128)(2,1)}, u32[]{:S(2)}, u32[]{:S(2)}) %collective-permute-start.2) | collective-permute-done | bytes 1966112 | tf_op jit(solution)/shard_map/ppermute | solution.py:18
  58.0 3.7 collective-permute-done.3
  61.7 5.3 %pad_maximum_fusion = bf16[160,160,128]{2,1,0:T(8,128)(2,1)} fusion(bf16[160,48,128]{2,1,0:T(8,128)(2,1)} %collective-permute-done.3, bf16[160,64,128]{2,1,0:T(8,128)(2,1)S(1)} %constant_dynamic-update-slice_fusion, bf16[160,48,128]{2,1,0:T(8,128)(2,1)} %collective-permute-done.2), kind=kLoop, calls=%fused_computation.29 | loop fusion | flops 19660800 | bytes 13107200 | tf_op jit(solution)/shard_map/concatenate | solution.py:22
  67.0 213.7 %while.13 = (s32[]{:T(128)}, bf16[16,4096]{1,0:T(8,128)(2,1)}, s32[16,3]{0,1:T(4,128)S(1)}, bf16[160,160,128]{2,1,0:T(8,128)(2,1)}, f32[96]{0:T(128)S(1)}, /*ind...) while((s32[]{:T(128)}, bf16[16,4096]{1,0:T(8,128)(2,1)}, ...), condition=%wide.region_2.3_spmd.clone.clone.clone, body=%wide.region_1.2_spmd.clone.clone.clone.sunk | while | flops 61371912 | bytes 3794567 | solution.py:91
  73.4 3.4 fusion.77
  76.7 1.7 convolution_bitcast_fusion.2
  86.7 3.4 fusion.77
  90.1 1.7 convolution_bitcast_fusion.2
  100.0 3.4 fusion.77
  103.4 1.7 convolution_bitcast_fusion.2
  113.4 3.4 fusion.77
  116.7 1.7 convolution_bitcast_fusion.2
  126.7 3.4 fusion.77
  130.1 1.7 convolution_bitcast_fusion.2
  140.1 3.4 fusion.77
  143.4 1.7 convolution_bitcast_fusion.2
  153.4 3.4 fusion.77
  156.8 1.7 convolution_bitcast_fusion.2
  166.7 3.4 fusion.77
  170.1 1.7 convolution_bitcast_fusion.2
  180.1 3.4 fusion.77
  183.4 1.7 convolution_bitcast_fusion.2
  193.4 3.4 fusion.77
  196.8 1.7 convolution_bitcast_fusion.2
  206.8 3.4 fusion.77
  210.1 1.7 convolution_bitcast_fusion.2
  220.1 3.4 fusion.77
  223.5 1.7 convolution_bitcast_fusion.2
  233.5 3.4 fusion.77
  236.8 1.7 convolution_bitcast_fusion.2
  246.8 3.4 fusion.77
  250.2 1.7 convolution_bitcast_fusion.2
  260.2 3.4 fusion.77
  263.5 1.7 convolution_bitcast_fusion.2
  273.5 3.4 fusion.77
  282.3 24.8 %all_gather.6 = bf16[256,256]{1,0:T(8,128)(2,1)S(1)} all-gather(bf16[16,256]{1,0:T(8,128)(2,1)S(1)} %select_convert_fusion), channel_id=1, replica_groups=mesh['tile'=16,'bank'=16] {'bank'}, dimensions={0}, use_global_device_ids=true | all-gather | bytes 139264 | tf_op jit(solution)/shard_map/all_gather | solution.py:101
  308.0 43.4 %all-gather.2.cloned.1.call-done = bf16[256,4096]{1,0:T(8,128)(2,1)} async-done(((bf16[16,4096]{1,0:T(8,128)(2,1)}), bf16[256,4096]{1,0:T(8,128)(2,1)}) %all-gather.2.cloned.1.call-update) | async-done | bytes 2097168 | tf_op jit(solution)/shard_map/all_gather | solution.py:100
  351.3 2.1 multiply_reduce_fusion.1
  353.4 4.0 convert_reduce_fusion
  357.5 3.7 fusion.32
  361.1 26.1 %psum.15 = f32[16,20]{1,0:T(8,128)} all-reduce(f32[16,20]{1,0:T(8,128)S(1)} %get-tuple-element.140), channel_id=1, replica_groups=mesh['tile'=16,'bank'=16] {'tile'}, use_global_device_ids=true, to_apply=%region_7.8 | all-reduce | flops 320 | bytes 2560 | tf_op jit(solution)/shard_map/psum | solution.py:104
  387.3 102.2 %all-reduce.2.cloned.1.call-done = f32[16,20,4096]{2,1,0:T(8,128)} async-done(((f32[16,20,4096]{2,1,0:T(8,128)}), f32[16,20,4096]{2,1,0:T(8,128)}) %all-reduce.2.cloned.1.call-update) | async-done | bytes 5242896 | tf_op jit(solution)/shard_map/psum | solution.py:104
  489.5 8.2 %copy.33 = f32[16,20,4096]{2,0,1:T(8,128)} copy(f32[16,20,4096]{2,1,0:T(8,128)} %all-reduce.2.cloned.1.call-done) | data formatting | bytes 10485760
  (136 shorter events, 51.0 us)
Async XLA Ops:
  7.2 344.2 %all-gather.2.cloned.1.call-start = ((), (), s32[]{:S(2)}) async-start(), calls=%async_computation | async-start | bytes 2228224 | tf_op jit(solution)/shard_map/all_gather | solution.py:100
  7.2 5.3 %copy-start.1 = (bf16[64,64,128]{2,1,0:T(8,128)(2,1)S(1)}, bf16[64,64,128]{2,1,0:T(8,128)(2,1)}, u32[]{:S(2)}) copy-start(bf16[64,64,128]{2,1,0:T(8,128)(2,1)} %param.8) | copy-start | bytes 3145732
  8.8 3.6 collective-permute-start
  10.6 5.8 %collective-permute-start.1 = (bf16[48,64,128]{2,1,0:T(8,128)(2,1)S(1)}, bf16[48,64,128]{2,1,0:T(8,128)(2,1)S(1)}, u32[]{:S(2)}, u32[]{:S(2)}) collective-permute-start(bf16[48,64,128]{2,1,0:T(8,128)(2,1)S(1)} %get-tuple-element.135), channel_id=1, source_target_pairs={{16,0},{32,16},{48,32},{64,48},{80,64},{96,80},{112,96},{128,112},... | collective-permute-start | bytes 2359304 | tf_op jit(solution)/shard_map/ppermute | solution.py:21
  16.5 9.8 %copy-start.5 = (s32[3,1,1,16]{3,2,1,0:T(1,128)S(1)}, s32[3,1,1,16]{3,2,1,0:T(1,128)}, u32[]{:S(2)}) copy-start(s32[3,1,1,16]{3,2,1,0:T(1,128)} %param.9) | copy-start | bytes 580
  19.2 38.8 %collective-permute-start.2 = (bf16[160,48,128]{2,1,0:T(8,128)(2,1)}, bf16[160,48,128]{2,1,0:T(8,128)(2,1)}, u32[]{:S(2)}, u32[]{:S(2)}) collective-permute-start(bf16[160,48,128]{2,1,0:T(8,128)(2,1)} %get-tuple-element.133), channel_id=1, source_target_pairs={{0,1},{1,2},{2,3},{3,4},{4,5},{5,6},{6,7},{7,8},{8,9},{9,10},{10,1... | collective-permute-start | bytes 5898248 | tf_op jit(solution)/shard_map/ppermute | solution.py:18
  22.6 39.1 %collective-permute-start.3 = (bf16[160,48,128]{2,1,0:T(8,128)(2,1)}, bf16[160,48,128]{2,1,0:T(8,128)(2,1)}, u32[]{:S(2)}, u32[]{:S(2)}) collective-permute-start(bf16[160,48,128]{2,1,0:T(8,128)(2,1)} %get-tuple-element.134), channel_id=1, source_target_pairs={{1,0},{2,1},{3,2},{4,3},{5,4},{6,5},{7,6},{8,7},{9,8},{10,9},{11,1... | collective-permute-start | bytes 5898248 | tf_op jit(solution)/shard_map/ppermute | solution.py:21
  67.0 214.4 %copy-start.4 = (s32[1,1,16,128]{3,2,1,0:T(8,128)S(1)}, s32[1,1,16,128]{3,2,1,0:T(8,128)}, u32[]{:S(2)}) copy-start(s32[1,1,16,128]{3,2,1,0:T(8,128)} %param.12) | copy-start | bytes 24580
  67.0 214.5 %copy-start.3 = (s32[1,1,16,128]{3,2,1,0:T(8,128)S(1)}, s32[1,1,16,128]{3,2,1,0:T(8,128)}, u32[]{:S(2)}) copy-start(s32[1,1,16,128]{3,2,1,0:T(8,128)} %param.11) | copy-start | bytes 24580
  67.0 240.2 %copy-start.2 = (bf16[16,20,4096]{2,0,1:T(8,128)(2,1)S(1)}, bf16[16,20,4096]{2,0,1:T(8,128)(2,1)}, u32[]{:S(2)}) copy-start(bf16[16,20,4096]{2,0,1:T(8,128)(2,1)} %param.13) | copy-start | bytes 7864324
  280.7 208.7 %all-reduce.2.cloned.1.call-start = ((), (), s32[]{:S(2)}) async-start(), calls=%async_computation.1 | async-start | bytes 12582912 | tf_op jit(solution)/shard_map/psum | solution.py:104
  353.4 4.0 copy-start
Sparse Core Ops, SparseCore 0:
  280.9 70.4 all-gather.1
  361.3 128.1 all-reduce.1
where the time goes:
time: 507 us; the launch traced here: 505 us
  waiting for transfers between devices  185 us (36%)
  matrix products  94.5 us (19%)
  loops' own time  88.9 us (18%)
  local copies, waits for them, and re-layouts  50.9 us (10%)
  blocking collectives  50.9 us (10%)
  between operations  14.9 us (3%)
  starting transfers between devices  10.3 us (2%)
  other arithmetic  8.83 us (2%)
    psum x1, waiting for transfers between devices, body(): class_sums, weight_sums = lax.psum((class_sums, weight_sums), 'tile')  102 us
    another operation x1, loops' own time, body(): features = lax.map(extract_one, coords)  88.9 us
    dot_general x16, matrix products, box_features(): jnp.dot(box_cube.reshape(B * B, B), table_half.T, preferred_element_type=...  53.8 us
    all_gather x1, waiting for transfers between devices, body(): lax.all_gather(features, 'bank', axis=0, tiled=True)  43.4 us
    ppermute x2, waiting for transfers between devices, extended(): lax.ppermute(lax.slice_in_dim(block, block.shape[dim] - width, None, axis...  32.1 us
    dot_general x16, matrix products, box_features(): jnp.einsum('xyc,by->xbc', first, table_full, precision=lax.Precision.HIGH...  27.1 us
    psum x1, blocking collectives, body(): class_sums, weight_sums = lax.psum((class_sums, weight_sums), 'tile')  26.1 us
    all_gather x1, blocking collectives, body(): lax.all_gather(multiplicity, 'bank', axis=0, tiled=True)  24.8 us
  transfers between devices with their start and end apart: 6, of which 6 were waited for; matrix products, arithmetic and copies ran while one was open for 0% of the time, Pallas kernels for 0%

commit v1 on v0

--- a/solution.py
+++ b/solution.py
@@ -97,7 +97,9 @@
     )
     multiplicity = jnp.where(live_slots[:, None], multiplicity, 0.0).astype(jnp.bfloat16)
     group_features, group_multiplicity = (
-        lax.all_gather(features, "bank", axis=0, tiled=True),
+        jnp.concatenate(
+            lax.all_to_all(jnp.stack([features] * lax.axis_size("bank")), "bank", 0, 0), axis=0
+        ),
         lax.all_gather(multiplicity, "bank", axis=0, tiled=True),
     )
     class_sums, weight_sums = score_local(group_features, group_multiplicity, reference_bank)

time: 507 us -> 492 us (0.970)
  waiting for transfers between devices: 185 us -> 145 us
  blocking collectives: 50.9 us -> 84.6 us
  local copies, waits for them, and re-layouts: 50.9 us -> 31.9 us
  starting transfers between devices: 10.3 us -> 19.8 us
    all_gather x1 -> x0, waiting for transfers between devices: 43.4 us -> none  [body(): lax.all_gather(features, 'bank', axis=0, tiled=True)]
    dynamic_update_slice x16, local copies, waits for them, and re-layouts: 24.3 us -> 3.65 us  [body(): features = lax.map(extract_one, coords)]
    psum x1, blocking collectives: 26.1 us -> 45.5 us  [body(): class_sums, weight_sums = lax.psum((class_sums, weight_sums), 'tile')]
    all_gather x1, blocking collectives: 24.8 us -> 39.1 us  [body(): lax.all_gather(multiplicity, 'bank', axis=0, tiled=True)]
    all_to_all x0 -> x1, starting transfers between devices: none -> 9.56 us  [body(): lax.all_to_all(jnp.stack([features] * lax.axis_size('bank')), 'bank', 0, 0)]
  transfers between devices with their start and end apart: 6 -> 6, of which waited for: 6 -> 5; matrix products, arithmetic and copies ran while one was open for 0% -> 1% of each run, Pallas kernels for 0% -> 0%
where the time goes in v1:
time: 492 us; the launch traced here: 489 us
  waiting for transfers between devices  145 us (29%)
  matrix products  94.6 us (19%)
  loops' own time  89.9 us (18%)
  blocking collectives  84.6 us (17%)
  local copies, waits for them, and re-layouts  31.9 us (6%)
  starting transfers between devices  19.8 us (4%)
  between operations  14.9 us (3%)
  other arithmetic  8.99 us (2%)
    psum x1, waiting for transfers between devices, body(): class_sums, weight_sums = lax.psum((class_sums, weight_sums), 'tile')  105 us
    another operation x1, loops' own time, body(): features = lax.map(extract_one, coords)  89.9 us
    dot_general x16, matrix products, box_features(): jnp.dot(box_cube.reshape(B * B, B), table_half.T, preferred_element_type=...  53.9 us
    psum x1, blocking collectives, body(): class_sums, weight_sums = lax.psum((class_sums, weight_sums), 'tile')  45.5 us
    all_gather x1, blocking collectives, body(): lax.all_gather(multiplicity, 'bank', axis=0, tiled=True)  39.1 us
    ppermute x2, waiting for transfers between devices, extended(): lax.ppermute(lax.slice_in_dim(block, block.shape[dim] - width, None, axis...  32.1 us
    dot_general x16, matrix products, box_features(): jnp.einsum('xyc,by->xbc', first, table_full, precision=lax.Precision.HIGH...  27.1 us
  transfers between devices with their start and end apart: 6, of which 5 were waited for; matrix products, arithmetic and copies ran while one was open for 1% of the time, Pallas kernels for 0%

profile of v1, /device:TPU:2, one launch (start us, length us, event | category | flops | bytes accessed | tf_op | source)
XLA Modules:
  0.0 489.4 jit_solution(227973970344860183)
XLA Ops:
  8.8 1.8 collective-permute-start
  12.6 3.8 collective-permute-done.1
  16.5 2.6 fusion.47
  19.1 3.4 collective-permute-start.2
  22.5 3.8 collective-permute-start.3
  26.4 31.6 %collective-permute-done.2 = bf16[160,48,128]{2,1,0:T(8,128)(2,1)} collective-permute-done((bf16[160,48,128]{2,1,0:T(8,128)(2,1)}, bf16[160,48,128]{2,1,0:T(8,128)(2,1)}, u32[]{:S(2)}, u32[]{:S(2)}) %collective-permute-start.2) | collective-permute-done | bytes 1966112 | tf_op jit(solution)/shard_map/ppermute | solution.py:18
  58.0 3.7 collective-permute-done.3
  61.6 5.3 %pad_maximum_fusion = bf16[160,160,128]{2,1,0:T(8,128)(2,1)} fusion(bf16[160,48,128]{2,1,0:T(8,128)(2,1)} %collective-permute-done.3, bf16[160,64,128]{2,1,0:T(8,128)(2,1)S(1)} %constant_dynamic-update-slice_fusion, bf16[160,48,128]{2,1,0:T(8,128)(2,1)} %collective-permute-done.2), kind=kLoop, calls=%fused_computation.29 | loop fusion | flops 19660800 | bytes 13107200 | tf_op jit(solution)/shard_map/concatenate | solution.py:22
  67.0 194.1 %while.13 = (s32[]{:T(128)}, bf16[16,4096]{1,0:T(8,128)(2,1)S(1)}, s32[16,3]{0,1:T(4,128)S(1)}, bf16[160,160,128]{2,1,0:T(8,128)(2,1)}, f32[96]{0:T(128)S(1)}, /...) while((s32[]{:T(128)}, bf16[16,4096]{1,0:T(8,128)(2,1)S(1)}, ...), condition=%wide.region_2.3_spmd.clone.clone.clone, body=%wide.region_1.2_spmd.clone.clone.clone.sunk | while | flops 61371912 | bytes 3794567 | solution.py:91
  73.2 3.4 fusion.69
  76.5 1.7 convolution_bitcast_fusion.2
  85.3 3.4 fusion.69
  88.7 1.7 convolution_bitcast_fusion.2
  97.4 3.4 fusion.69
  100.8 1.7 convolution_bitcast_fusion.2
  109.6 3.4 fusion.69
  112.9 1.7 convolution_bitcast_fusion.2
  121.7 3.4 fusion.69
  125.1 1.7 convolution_bitcast_fusion.2
  133.8 3.4 fusion.69
  137.2 1.7 convolution_bitcast_fusion.2
  146.0 3.4 fusion.69
  149.3 1.7 convolution_bitcast_fusion.2
  158.1 3.4 fusion.69
  161.5 1.7 convolution_bitcast_fusion.2
  170.2 3.4 fusion.69
  173.6 1.7 convolution_bitcast_fusion.2
  182.4 3.4 fusion.69
  185.7 1.7 convolution_bitcast_fusion.2
  194.5 3.4 fusion.69
  197.9 1.7 convolution_bitcast_fusion.2
  206.6 3.4 fusion.69
  210.0 1.7 convolution_bitcast_fusion.2
  218.8 3.4 fusion.69
  222.1 1.7 convolution_bitcast_fusion.2
  230.9 3.4 fusion.69
  234.3 1.7 convolution_bitcast_fusion.2
  243.0 3.4 fusion.69
  246.4 1.7 convolution_bitcast_fusion.2
  255.2 3.4 fusion.69
  262.7 9.6 %all-to-all-start = ((bf16[16,16,4096]{2,1,0:T(8,128)(2,1)}), bf16[16,16,4096]{2,1,0:T(8,128)(2,1)S(1)}, u32[]{:S(2)}, u32[]{:S(2)}) async-start(bf16[16,16,4096]{2,1,0:T(8,128)(2,1)} %stack.5), calls=%async_computation | async-start | bytes 4194304 | tf_op jit(solution)/shard_map/all_to_all | solution.py:101
  273.7 39.1 %all_gather.3 = bf16[256,256]{1,0:T(8,128)(2,1)S(1)} all-gather(bf16[16,256]{1,0:T(8,128)(2,1)S(1)} %select_convert_fusion), channel_id=1, replica_groups=mesh['tile'=16,'bank'=16] {'bank'}, dimensions={0}, use_global_device_ids=true | all-gather | bytes 139264 | tf_op jit(solution)/shard_map/all_gather | solution.py:103
  313.1 2.3 multiply_reduce_fusion
  316.1 4.0 convert_reduce_fusion
  320.1 3.7 fusion.49
  323.8 45.5 %psum.15 = f32[16,20]{1,0:T(8,128)} all-reduce(f32[16,20]{1,0:T(8,128)S(1)} %get-tuple-element.140), channel_id=1, replica_groups=mesh['tile'=16,'bank'=16] {'tile'}, use_global_device_ids=true, to_apply=%region_7.8 | all-reduce | flops 320 | bytes 2560 | tf_op jit(solution)/shard_map/psum | solution.py:106
  369.3 105.0 %all-reduce.2.cloned.1.call-done = f32[16,20,4096]{2,1,0:T(8,128)} async-done(((f32[16,20,4096]{2,1,0:T(8,128)}), f32[16,20,4096]{2,1,0:T(8,128)}) %all-reduce.2.cloned.1.call-update) | async-done | bytes 5242896 | tf_op jit(solution)/shard_map/psum | solution.py:106
  474.3 8.2 %copy.33 = f32[16,20,4096]{2,0,1:T(8,128)} copy(f32[16,20,4096]{2,1,0:T(8,128)} %all-reduce.2.cloned.1.call-done) | data formatting | bytes 10485760
  (133 shorter events, 32.0 us)
Async XLA Ops:
  7.2 5.3 %copy-start = (bf16[64,64,128]{2,1,0:T(8,128)(2,1)S(1)}, bf16[64,64,128]{2,1,0:T(8,128)(2,1)}, u32[]{:S(2)}) copy-start(bf16[64,64,128]{2,1,0:T(8,128)(2,1)} %param.8) | copy-start | bytes 3145732
  8.8 3.6 collective-permute-start
  10.6 5.8 %collective-permute-start.1 = (bf16[48,64,128]{2,1,0:T(8,128)(2,1)S(1)}, bf16[48,64,128]{2,1,0:T(8,128)(2,1)S(1)}, u32[]{:S(2)}, u32[]{:S(2)}) collective-permute-start(bf16[48,64,128]{2,1,0:T(8,128)(2,1)S(1)} %get-tuple-element.135), channel_id=1, source_target_pairs={{16,0},{32,16},{48,32},{64,48},{80,64},{96,80},{112,96},{128,112},... | collective-permute-start | bytes 2359304 | tf_op jit(solution)/shard_map/ppermute | solution.py:21
  16.5 9.8 %copy-start.3 = (s32[3,1,1,16]{3,2,1,0:T(1,128)S(1)}, s32[3,1,1,16]{3,2,1,0:T(1,128)}, u32[]{:S(2)}) copy-start(s32[3,1,1,16]{3,2,1,0:T(1,128)} %param.9) | copy-start | bytes 580
  19.1 38.8 %collective-permute-start.2 = (bf16[160,48,128]{2,1,0:T(8,128)(2,1)}, bf16[160,48,128]{2,1,0:T(8,128)(2,1)}, u32[]{:S(2)}, u32[]{:S(2)}) collective-permute-start(bf16[160,48,128]{2,1,0:T(8,128)(2,1)} %get-tuple-element.133), channel_id=1, source_target_pairs={{0,1},{1,2},{2,3},{3,4},{4,5},{5,6},{6,7},{7,8},{8,9},{9,10},{10,1... | collective-permute-start | bytes 5898248 | tf_op jit(solution)/shard_map/ppermute | solution.py:18
  22.5 39.1 %collective-permute-start.3 = (bf16[160,48,128]{2,1,0:T(8,128)(2,1)}, bf16[160,48,128]{2,1,0:T(8,128)(2,1)}, u32[]{:S(2)}, u32[]{:S(2)}) collective-permute-start(bf16[160,48,128]{2,1,0:T(8,128)(2,1)} %get-tuple-element.134), channel_id=1, source_target_pairs={{1,0},{2,1},{3,2},{4,3},{5,4},{6,5},{7,6},{8,7},{9,8},{10,9},{11,1... | collective-permute-start | bytes 5898248 | tf_op jit(solution)/shard_map/ppermute | solution.py:21
  262.7 10.3 %copy-start.2 = (s32[1,1,16,128]{3,2,1,0:T(8,128)S(1)}, s32[1,1,16,128]{3,2,1,0:T(8,128)}, u32[]{:S(2)}) copy-start(s32[1,1,16,128]{3,2,1,0:T(8,128)} %param.12) | copy-start | bytes 24580
  262.7 10.3 %copy-start.1 = (s32[1,1,16,128]{3,2,1,0:T(8,128)S(1)}, s32[1,1,16,128]{3,2,1,0:T(8,128)}, u32[]{:S(2)}) copy-start(s32[1,1,16,128]{3,2,1,0:T(8,128)} %param.11) | copy-start | bytes 24580
  262.7 52.8 %all-to-all-start = ((bf16[16,16,4096]{2,1,0:T(8,128)(2,1)}), bf16[16,16,4096]{2,1,0:T(8,128)(2,1)S(1)}, u32[]{:S(2)}, u32[]{:S(2)}) async-start(bf16[16,16,4096]{2,1,0:T(8,128)(2,1)} %stack.5), calls=%async_computation | async-start | bytes 4194304 | tf_op jit(solution)/shard_map/all_to_all | solution.py:101
  272.2 202.1 %all-reduce.2.cloned.1.call-start = ((), (), s32[]{:S(2)}) async-start(), calls=%async_computation.1 | async-start | bytes 12582912 | tf_op jit(solution)/shard_map/psum | solution.py:106
Sparse Core Ops, SparseCore 0:
  323.9 150.3 all-reduce.1
